TPU v7x, 256 devices: a whole 4x4x8 slice. The times are simulated.
256 devices in a mesh: segment: 4 (over x_lo, core), dp: 64 (over z, x_hi, y).
Axes of the slice: x: 4 (x_hi: 2, x_lo: 2; x = x_hi * 2 + x_lo), y: 4, z: 8, core: 2. Of those that a mesh axis runs over, the one named last changes fastest.
Arguments:
- latents: bfloat16 [128, 16, 16, 320], P('dp'), may hold values from -6 to 6
- cotangent: bfloat16 [128, 16, 16, 320], P('dp'), may hold values from -6 to 6
- bucket: int32 [128, 2], P('dp'), may hold values from 8 to 16, as said below
- timesteps: int32 [128], P('dp'), may hold values from 0 to 999
- w_enc: bfloat16 [4, 3, 3, 320, 320], P('segment'), may hold values from -0.109375 to 0.109375
- w_dec: bfloat16 [4, 3, 3, 320, 320], P('segment'), may hold values from -0.109375 to 0.109375
- w_time: bfloat16 [4, 2, 320, 320], P('segment'), may hold values from -0.3125 to 0.3125
Outputs:
- grad_enc: float32 [4, 3, 3, 320, 320], P('segment')
- grad_dec: float32 [4, 3, 3, 320, 320], P('segment')
Inputs may be any that keep to these rules, and one draw needn't show every extreme that they name: `bucket`: row b holds the height and width of the valid region at the start of microbatch b's 16 x 16 crop; in every draw some microbatch is 16 x 16 and another 16 // 2 x 16 // 2.
All inputs are finite; a program needn't handle non-finite values.
Results may differ from a plain program's by a relative error of at most 0.018.
Values may be sent and summed in bfloat16 or wider, within the bound.
No kernel may reach another device: no remote copies, remote signals or barrier semaphores. Data moves between devices by JAX's collectives and lax.ppermute only.
A program may use at most 128 MiB of HBM per device.

v0:
```python
import math

import jax
import jax.numpy as jnp
from jax import lax
from jax.sharding import PartitionSpec as P

G = 32


def from_behind(value, axis, steps):
    count = lax.axis_size(axis)
    first, last = (max(0, -steps), min(count, count - steps))
    return lax.ppermute(value, axis, [(source, source + steps) for source in range(first, last)])


def crop_mask(bucket, side):
    row_index = jnp.arange(side, dtype=jnp.int32)
    inside = (row_index[None, :, None] < bucket[:, 0, None, None]) & (
        row_index[None, None, :] < bucket[:, 1, None, None]
    )
    return inside.astype(jnp.float32)


def time_embed(timesteps, embed_width):
    half_width = embed_width // 2
    frequencies = jnp.exp(
        -math.log(10000.0) * jnp.arange(half_width, dtype=jnp.float32) / half_width
    )
    angles = timesteps.astype(jnp.float32)[:, None] * frequencies[None, :]
    return jnp.concatenate([jnp.cos(angles), jnp.sin(angles)], axis=1).astype(jnp.bfloat16)


def prepare(values, cell_mask, temb, groups):
    count_n, side, other_side, width = values.shape
    grouped = values.reshape(count_n, side, other_side, groups, width // groups)
    weighting = cell_mask[:, :, :, None, None]
    entries = jnp.sum(cell_mask, axis=(1, 2)) * (width // groups)
    group_mean = jnp.sum(grouped * weighting, axis=(1, 2, 4)) / entries[:, None]
    centered = grouped - group_mean[:, None, None, :, None]
    group_var = jnp.sum(centered * centered * weighting, axis=(1, 2, 4)) / entries[:, None]
    normed = (centered * lax.rsqrt(group_var + 1e-05)[:, None, None, :, None]).reshape(
        count_n, side, other_side, width
    )
    return jax.nn.silu(normed + temb[:, None, None, :]) * cell_mask[..., None]


def conv_apply(hidden, kernel):
    return lax.conv_general_dilated(
        hidden,
        kernel,
        (1, 1),
        "SAME",
        dimension_numbers=("NHWC", "HWIO", "NHWC"),
        preferred_element_type=jnp.float32,
    )


def block_forward(values, cell_mask, temb, kernel, groups):
    hidden = prepare(values, cell_mask, temb, groups).astype(jnp.bfloat16)
    result = ((values + conv_apply(hidden, kernel)) * cell_mask[..., None]).astype(jnp.bfloat16)
    return (result, hidden)


def block_backward(values, cell_mask, temb, kernel, cot_out, groups):
    residual_cot = cot_out.astype(jnp.float32) * cell_mask[..., None]
    cot_conv = residual_cot.astype(jnp.bfloat16)
    flipped = jnp.transpose(kernel[::-1, ::-1], (0, 1, 3, 2))
    hidden_cot = conv_apply(cot_conv, flipped)
    primal, pull_back = jax.vjp(lambda inner: prepare(inner, cell_mask, temb, groups), values)
    return (residual_cot + pull_back(hidden_cot)[0], cot_conv)


def weight_grad(hidden, cot_conv):
    side = hidden.shape[1]
    width = hidden.shape[3]
    flat_cot = cot_conv.reshape(-1, cot_conv.shape[3])
    padded = jnp.pad(hidden, ((0, 0), (1, 1), (1, 1), (0, 0)))
    rows_list = []
    for row_shift in range(3):
        across = []
        for col_shift in range(3):
            window = padded[
                :, row_shift : row_shift + side, col_shift : col_shift + side, :
            ].reshape(-1, width)
            across.append(
                lax.dot_general(
                    window, flat_cot, (((0,), (0,)), ((), ())), preferred_element_type=jnp.float32
                )
            )
        rows_list.append(jnp.stack(across))
    return jnp.stack(rows_list)


def item(array, slot):
    return lax.dynamic_index_in_dim(array, slot, 0, keepdims=True)


def store(buffer, value, slot, active):
    former = lax.dynamic_index_in_dim(buffer, slot, 0, keepdims=False)
    return lax.dynamic_update_index_in_dim(buffer, jnp.where(active, value, former), slot, 0)


def to_last(values):
    return from_behind(values, "segment", 1)


def to_first(values):
    return from_behind(values, "segment", -1)


def local(latents, cotangent, bucket, timesteps, w_enc, w_dec, w_time):
    section = lax.axis_index("segment")
    sections = lax.axis_size("segment")
    micro_count = latents.shape[0]
    side = latents.shape[1]
    width = latents.shape[3]
    ticks = micro_count + sections - 1
    is_first = section == 0
    is_last = section == sections - 1
    cell_mask = crop_mask(bucket, side)
    embedding = time_embed(timesteps, w_time.shape[2])
    temb_enc = jnp.dot(embedding, w_time[0, 0], preferred_element_type=jnp.float32)
    temb_dec = jnp.dot(embedding, w_time[0, 1], preferred_element_type=jnp.float32)
    loss_scale = float(micro_count * lax.axis_size("dp") * side * side) ** (-0.5)
    kernel_enc = w_enc[0]
    kernel_dec = w_dec[0]
    zero_acts = jnp.zeros((micro_count, side, side, width), jnp.bfloat16)
    single = jnp.zeros((side, side, width), jnp.bfloat16)
    zero_grad = jnp.zeros((3, 3, width, width), jnp.float32)

    def pick(tick_index, offset):
        wanted = tick_index - offset
        active = (wanted >= 0) & (wanted < micro_count)
        return (jnp.clip(wanted, 0, micro_count - 1), active)

    def enc_tick(tick_index, loop_state):
        incoming, enc_inputs, enc_hidden, enc_results = loop_state
        slot, active = pick(tick_index, section)
        inputs = jnp.where(is_first, item(latents, slot)[0], incoming)
        result, hidden = block_forward(
            inputs.astype(jnp.float32)[None],
            item(cell_mask, slot),
            item(temb_enc, slot),
            kernel_enc,
            G,
        )
        enc_inputs = store(enc_inputs, inputs, slot, active)
        enc_hidden = store(enc_hidden, hidden[0], slot, active)
        enc_results = store(enc_results, result[0], slot, active)
        return (to_last(result[0]), enc_inputs, enc_hidden, enc_results)

    loop_state = lax.fori_loop(0, ticks, enc_tick, (single, zero_acts, zero_acts, zero_acts))
    enc_inputs, enc_hidden, enc_results = (loop_state[1], loop_state[2], loop_state[3])

    def dec_tick(tick_index, loop_state):
        incoming, dec_upper, dec_hidden = loop_state
        slot, active = pick(tick_index, sections - 1 - section)
        upper = jnp.where(is_last, item(enc_results, slot)[0], incoming)
        summed = upper.astype(jnp.float32)[None] + item(enc_inputs, slot).astype(jnp.float32)
        result, hidden = block_forward(
            summed, item(cell_mask, slot), item(temb_dec, slot), kernel_dec, G
        )
        dec_upper = store(dec_upper, upper, slot, active)
        dec_hidden = store(dec_hidden, hidden[0], slot, active)
        return (to_first(result[0]), dec_upper, dec_hidden)

    loop_state = lax.fori_loop(0, ticks, dec_tick, (single, zero_acts, zero_acts))
    dec_upper, dec_hidden = (loop_state[1], loop_state[2])

    def dec_back_tick(tick_index, loop_state):
        incoming, skip_cot, accum = loop_state
        slot, active = pick(tick_index, section)
        start = (item(cotangent, slot)[0].astype(jnp.float32) * loss_scale).astype(jnp.bfloat16)
        cot_here = jnp.where(is_first, start, incoming)
        summed = item(dec_upper, slot).astype(jnp.float32) + item(enc_inputs, slot).astype(
            jnp.float32
        )
        grad_in, cot_conv = block_backward(
            summed, item(cell_mask, slot), item(temb_dec, slot), kernel_dec, cot_here[None], G
        )
        accum = accum + jnp.where(active, weight_grad(item(dec_hidden, slot), cot_conv), 0.0)
        sent = grad_in[0].astype(jnp.bfloat16)
        skip_cot = store(skip_cot, sent, slot, active)
        return (to_last(sent), skip_cot, accum)

    loop_state = lax.fori_loop(0, ticks, dec_back_tick, (single, zero_acts, zero_grad))
    skip_cot = loop_state[1]
    grad_dec = loop_state[2]

    def enc_back_tick(tick_index, loop_state):
        incoming, accum = loop_state
        slot, active = pick(tick_index, sections - 1 - section)
        skip_here = item(skip_cot, slot)[0]
        cot_here = jnp.where(is_last, skip_here, incoming)
        grad_in, cot_conv = block_backward(
            item(enc_inputs, slot).astype(jnp.float32),
            item(cell_mask, slot),
            item(temb_enc, slot),
            kernel_enc,
            cot_here[None],
            G,
        )
        accum = accum + jnp.where(active, weight_grad(item(enc_hidden, slot), cot_conv), 0.0)
        sent = (grad_in[0] + skip_here.astype(jnp.float32)).astype(jnp.bfloat16)
        return (to_first(sent), accum)

    loop_state = lax.fori_loop(0, ticks, enc_back_tick, (single, zero_grad))
    grad_enc = loop_state[1]
    summed_enc, summed_dec = lax.psum((grad_enc, grad_dec), "dp")
    return (summed_enc[None], summed_dec[None])


def solution(mesh):
    placed = (
        P("dp", None, None, None),
        P("dp", None, None, None),
        P("dp", None),
        P("dp"),
        P("segment", None, None, None, None),
        P("segment", None, None, None, None),
        P("segment", None, None, None),
    )
    return jax.shard_map(
        local,
        mesh=mesh,
        in_specs=placed,
        out_specs=(P("segment", None, None, None, None), P("segment", None, None, None, None)),
        check_vma=False,
    )
```

profile of v0, /device:TPU:2, one launch (start us, length us, event | category | flops | bytes accessed | tf_op | source)
XLA Modules:
  0.0 1145.4 jit_solution(1794802183554280157)
XLA Ops:
  11.6 71.0 %while.76 = (s32[]{:T(128)}, bf16[16,16,320]{2,0,1:T(8,128)(2,1)S(1)}, bf16[2,16,16,320]{3,1,2,0:T(8,128)(2,1)S(1)}, bf16[2,16,16,320]{3,1,2,0:T(8,128)(2,1)S(1)...) while((s32[]{:T(128)}, ...), condition=%wide.region_6.7_spmd, body=%wide.region_0.6_spmd.sunk | while | flops 682516800 | bytes 9471447 | solution.py:153
  20.8 5.1 collective-permute-done
  35.0 5.1 collective-permute-done
  49.2 5.1 collective-permute-done
  63.3 5.1 collective-permute-done
  77.5 5.1 collective-permute-done
  83.4 62.2 %while.77 = (s32[]{:T(128)}, bf16[16,16,320]{2,0,1:T(8,128)(2,1)S(1)}, bf16[2,16,16,320]{3,1,2,0:T(8,128)(2,1)S(1)}, bf16[2,16,16,320]{3,1,2,0:T(8,128)(2,1)S(1)...) while((s32[]{:T(128)}, ...), condition=%wide.region_13.14_spmd, body=%wide.region_7.13_spmd.sunk | while | flops 682352960 | bytes 16733947 | solution.py:168
  100.1 3.8 collective-permute-start.1
  112.9 3.8 collective-permute-start.1
  125.7 3.8 collective-permute-start.1
  138.6 3.8 collective-permute-start.1
  145.6 130.8 %while.78 = (s32[]{:T(128)}, bf16[16,16,320]{2,0,1:T(8,128)(2,1)S(1)}, bf16[2,16,16,320]{3,1,2,0:T(8,128)(2,1)S(1)}, f32[3,3,320,320]{3,2,1,0:T(8,128)}, pred[]{...) while((s32[]{:T(128)}, ...), condition=%wide.region_24.25_spmd.clone, body=%wide.region_14.0_spmd.clone.sunk | while | flops 1163448832 | bytes 44409040 | solution.py:187
  149.4 3.2 convolution_select_fusion.10
  173.7 3.2 convolution_select_fusion.10
  191.6 5.0 fusion.298
  200.4 3.2 convolution_select_fusion.10
  218.2 5.0 fusion.298
  244.8 5.0 fusion.298
  271.4 5.0 fusion.298
  276.4 122.6 %while.79 = (s32[]{:T(128)}, bf16[16,16,320]{2,0,1:T(8,128)(2,1)S(1)}, f32[3,3,320,320]{3,2,1,0:T(8,128)}, pred[]{:T(512)}, s32[]{:T(128)}, /*index=5*/bf16[2,16...) while((s32[]{:T(128)}, ...), condition=%wide.region_35.36_spmd.clone, body=%wide.region_25.35_spmd.clone.sunk | while | flops 1162220032 | bytes 39374832 | solution.py:208
  277.6 3.2 convolution_select_fusion.11
  284.9 3.8 collective-permute-start.3
  301.7 3.2 convolution_select_fusion.11
  320.7 5.0 fusion.326
  326.6 3.2 convolution_select_fusion.11
  345.1 5.0 fusion.326
  351.1 3.2 convolution_select_fusion.11
  369.6 5.0 fusion.326
  375.5 3.2 convolution_select_fusion.11
  394.0 5.0 fusion.326
  399.1 732.6 %all-reduce.5.cloned.1.call-done = (f32[1,3,3,320,320]{4,3,2,1,0:T(8,128)}, f32[1,3,3,320,320]{4,3,2,1,0:T(8,128)}) async-done(((f32[1,3,3,320,320]{4,3,2,1,0:T(8,128)}, f32[1,3,3,320,320]{4,3,2,1,0:T(8,128)}), (f32[1,3,3,320,320]{4,3,2,1,0:T(8,128)}, f32[1,3,3,320,320]{4,3,2,1,0:T(8,128)})) %all-reduce.5.cloned.1.call-update) | async-done | bytes 7372816 | tf_op jit(solution)/shard_map/psum | solution.py:210
  1131.7 4.8 copy.223
  (908 shorter events, 266.9 us)
Async XLA Ops:
  7.2 1124.5 %all-reduce.5.cloned.1.call-start = ((), (), s32[]{:S(2)}) async-start(), calls=%async_computation | async-start | bytes 17694720 | tf_op jit(solution)/shard_map/psum | solution.py:210
  18.9 7.0 collective-permute-start
  33.0 7.0 collective-permute-start
  47.2 7.0 collective-permute-start
  61.4 7.0 collective-permute-start
  75.6 7.0 collective-permute-start
  89.2 5.1 collective-permute-start.1
  100.1 7.0 collective-permute-start.1
  112.9 7.0 collective-permute-start.1
  125.7 7.0 collective-permute-start.1
  138.6 7.0 collective-permute-start.1
  145.6 130.8 %copy-start.1 = (bf16[2,16,16,320]{3,1,2,0:T(8,128)(2,1)S(1)}, bf16[2,16,16,320]{3,1,2,0:T(8,128)(2,1)}, u32[]{:S(2)}) copy-start(bf16[2,16,16,320]{3,1,2,0:T(8,128)(2,1)} %copy-done) | copy-start | bytes 983044
  145.6 7.1 copy-start.12
  155.1 14.9 %collective-permute-start.2 = (bf16[16,16,320]{2,0,1:T(8,128)(2,1)}, bf16[16,16,320]{2,0,1:T(8,128)(2,1)S(1)}, u32[]{:S(2)}, u32[]{:S(2)}) collective-permute-start(bf16[16,16,320]{2,0,1:T(8,128)(2,1)} %get-tuple-element.1589), channel_id=1, source_target_pairs={{0,64},{64,128},{128,192},{1,65},{65,129},{129,193},{2,66},{66,130... | collective-permute-start | bytes 491528 | tf_op jit(solution)/shard_map/while/body/eval_jaxpr/ppermute | solution.py:14
  170.0 7.1 copy-start.12
  179.4 17.2 %collective-permute-start.2 = (bf16[16,16,320]{2,0,1:T(8,128)(2,1)}, bf16[16,16,320]{2,0,1:T(8,128)(2,1)S(1)}, u32[]{:S(2)}, u32[]{:S(2)}) collective-permute-start(bf16[16,16,320]{2,0,1:T(8,128)(2,1)} %get-tuple-element.1589), channel_id=1, source_target_pairs={{0,64},{64,128},{128,192},{1,65},{65,129},{129,193},{2,66},{66,130... | collective-permute-start | bytes 491528 | tf_op jit(solution)/shard_map/while/body/eval_jaxpr/ppermute | solution.py:14
  196.6 7.1 copy-start.12
  206.0 17.2 %collective-permute-start.2 = (bf16[16,16,320]{2,0,1:T(8,128)(2,1)}, bf16[16,16,320]{2,0,1:T(8,128)(2,1)S(1)}, u32[]{:S(2)}, u32[]{:S(2)}) collective-permute-start(bf16[16,16,320]{2,0,1:T(8,128)(2,1)} %get-tuple-element.1589), channel_id=1, source_target_pairs={{0,64},{64,128},{128,192},{1,65},{65,129},{129,193},{2,66},{66,130... | collective-permute-start | bytes 491528 | tf_op jit(solution)/shard_map/while/body/eval_jaxpr/ppermute | solution.py:14
  223.2 7.1 copy-start.12
  232.6 17.2 %collective-permute-start.2 = (bf16[16,16,320]{2,0,1:T(8,128)(2,1)}, bf16[16,16,320]{2,0,1:T(8,128)(2,1)S(1)}, u32[]{:S(2)}, u32[]{:S(2)}) collective-permute-start(bf16[16,16,320]{2,0,1:T(8,128)(2,1)} %get-tuple-element.1589), channel_id=1, source_target_pairs={{0,64},{64,128},{128,192},{1,65},{65,129},{129,193},{2,66},{66,130... | collective-permute-start | bytes 491528 | tf_op jit(solution)/shard_map/while/body/eval_jaxpr/ppermute | solution.py:14
  249.8 7.1 copy-start.12
  259.2 17.2 %collective-permute-start.2 = (bf16[16,16,320]{2,0,1:T(8,128)(2,1)}, bf16[16,16,320]{2,0,1:T(8,128)(2,1)S(1)}, u32[]{:S(2)}, u32[]{:S(2)}) collective-permute-start(bf16[16,16,320]{2,0,1:T(8,128)(2,1)} %get-tuple-element.1589), channel_id=1, source_target_pairs={{0,64},{64,128},{128,192},{1,65},{65,129},{129,193},{2,66},{66,130... | collective-permute-start | bytes 491528 | tf_op jit(solution)/shard_map/while/body/eval_jaxpr/ppermute | solution.py:14
  277.6 5.1 copy-start.11
  284.9 15.9 %collective-permute-start.3 = (bf16[16,16,320]{2,0,1:T(8,128)(2,1)}, bf16[16,16,320]{2,0,1:T(8,128)(2,1)S(1)}, u32[]{:S(2)}, u32[]{:S(2)}) collective-permute-start(bf16[16,16,320]{2,0,1:T(8,128)(2,1)} %fusion.325), channel_id=1, source_target_pairs={{64,0},{128,64},{192,128},{65,1},{129,65},{193,129},{66,2},{130,66... | collective-permute-start | bytes 491528 | tf_op jit(solution)/shard_map/while/body/eval_jaxpr/ppermute | solution.py:14
  301.7 5.1 copy-start.11
  309.0 16.7 %collective-permute-start.3 = (bf16[16,16,320]{2,0,1:T(8,128)(2,1)}, bf16[16,16,320]{2,0,1:T(8,128)(2,1)S(1)}, u32[]{:S(2)}, u32[]{:S(2)}) collective-permute-start(bf16[16,16,320]{2,0,1:T(8,128)(2,1)} %fusion.325), channel_id=1, source_target_pairs={{64,0},{128,64},{192,128},{65,1},{129,65},{193,129},{66,2},{130,66... | collective-permute-start | bytes 491528 | tf_op jit(solution)/shard_map/while/body/eval_jaxpr/ppermute | solution.py:14
  326.6 5.1 copy-start.11
  333.9 16.2 %collective-permute-start.3 = (bf16[16,16,320]{2,0,1:T(8,128)(2,1)}, bf16[16,16,320]{2,0,1:T(8,128)(2,1)S(1)}, u32[]{:S(2)}, u32[]{:S(2)}) collective-permute-start(bf16[16,16,320]{2,0,1:T(8,128)(2,1)} %fusion.325), channel_id=1, source_target_pairs={{64,0},{128,64},{192,128},{65,1},{129,65},{193,129},{66,2},{130,66... | collective-permute-start | bytes 491528 | tf_op jit(solution)/shard_map/while/body/eval_jaxpr/ppermute | solution.py:14
  351.1 5.1 copy-start.11
  358.4 16.2 %collective-permute-start.3 = (bf16[16,16,320]{2,0,1:T(8,128)(2,1)}, bf16[16,16,320]{2,0,1:T(8,128)(2,1)S(1)}, u32[]{:S(2)}, u32[]{:S(2)}) collective-permute-start(bf16[16,16,320]{2,0,1:T(8,128)(2,1)} %fusion.325), channel_id=1, source_target_pairs={{64,0},{128,64},{192,128},{65,1},{129,65},{193,129},{66,2},{130,66... | collective-permute-start | bytes 491528 | tf_op jit(solution)/shard_map/while/body/eval_jaxpr/ppermute | solution.py:14
  375.5 5.1 copy-start.11
  382.9 16.2 %collective-permute-start.3 = (bf16[16,16,320]{2,0,1:T(8,128)(2,1)}, bf16[16,16,320]{2,0,1:T(8,128)(2,1)S(1)}, u32[]{:S(2)}, u32[]{:S(2)}) collective-permute-start(bf16[16,16,320]{2,0,1:T(8,128)(2,1)} %fusion.325), channel_id=1, source_target_pairs={{64,0},{128,64},{192,128},{65,1},{129,65},{193,129},{66,2},{130,66... | collective-permute-start | bytes 491528 | tf_op jit(solution)/shard_map/while/body/eval_jaxpr/ppermute | solution.py:14
  (69 other events, 157.3 us)
Sparse Core Ops, SparseCore 0:
  399.2 732.4 all-reduce.4
where the time goes:
time: 1150 us
  waiting for transfers between devices  774 us (67%)
  matrix products  131 us (11%)
  other arithmetic  110 us (10%)
  local copies, waits for them, and re-layouts  51.4 us (4%)
  starting transfers between devices  48.3 us (4%)
  loops' own time  16.9 us (1%)
  between operations  14.1 us (1%)
    psum x1, waiting for transfers between devices, local(): summed_enc, summed_dec = lax.psum((grad_enc, grad_dec), 'dp')  733 us
    dot_general x90, matrix products, weight_grad(): lax.dot_general(window, flat_cot, (((0,), (0,)), ((), ())), preferred_ele...  75.9 us
    conv_general_dilated x20, matrix products, conv_apply(): lax.conv_general_dilated(hidden, kernel, (1, 1), 'SAME', dimension_number...  53.3 us
    ppermute x20, starting transfers between devices, from_behind(): lax.ppermute(value, axis, [(source, source + steps) for source in range(f...  48.2 us
    ppermute x20, waiting for transfers between devices, from_behind(): lax.ppermute(value, axis, [(source, source + steps) for source in range(f...  41.1 us
  transfers between devices with their start and end apart: 21, of which 11 were waited for; matrix products, arithmetic and copies ran while one was open for 12% of the time, Pallas kernels for 0%

commit v1 on v0

v1 whole, which is shorter than its diff:
```python
import functools
import math

import jax
import jax.numpy as jnp
import numpy as np
from jax import lax
from jax.experimental import pallas as pl
from jax.experimental.layout import Layout, with_layout_constraint
from jax.experimental.pallas import tpu as pltpu
from jax.sharding import Mesh, PartitionSpec as P

G = 32
SIDE = 16
CELLS = SIDE * SIDE
C = 320
TAPS = 3 * C
F32 = jnp.float32
BF16 = jnp.bfloat16
VMEM_LIMIT = 40 * 1024 * 1024
LANES = 128
FLAT = 9 * C
TAIL = C - 2 * LANES
PACKED_USED = 2 * FLAT + FLAT // 2
PACKED = 64 * 128

NT = (((1,), (1,)), ((), ()))


def group_matrix():
    index = np.arange(C) // (C // G)
    return jnp.asarray((index[:, None] == index[None, :]).astype(np.float32), BF16)


def group_sums(columns, matrix):
    row = lax.broadcasted_iota(jnp.int32, (16, C), 0)
    stacked = jnp.zeros((16, C), F32)
    for at, column in enumerate(columns):
        high = column.astype(BF16).astype(F32)
        rest = column - high
        middle = rest.astype(BF16).astype(F32)
        low = (rest - middle).astype(BF16).astype(F32)
        for part, value in enumerate((high, middle, low)):
            stacked = jnp.where(row == 3 * at + part, value, stacked)
    sums = jnp.dot(stacked.astype(BF16), matrix, preferred_element_type=F32)
    return [
        sums[3 * at : 3 * at + 1] + sums[3 * at + 1 : 3 * at + 2] + sums[3 * at + 2 : 3 * at + 3]
        for at in range(len(columns))
    ]


def col_sum(values):
    return jnp.sum(values, axis=0, keepdims=True)


def column_index():
    return lax.broadcasted_iota(jnp.int32, (CELLS, C), 0) % SIDE


def shift_right(values, column):
    return jnp.where(column == 0, 0.0, pltpu.roll(values, 1, axis=0))


def shift_left(values, column):
    return jnp.where(column == SIDE - 1, 0.0, pltpu.roll(values, CELLS - 1, axis=0))


def clear_edges(padded):
    width = padded.shape[1]
    padded[0:SIDE, :] = jnp.zeros((SIDE, width), BF16)
    padded[SIDE + CELLS :, :] = jnp.zeros((SIDE, width), BF16)


def store_windows(padded, hidden, column):
    padded[SIDE : SIDE + CELLS, 0:C] = shift_right(hidden, column).astype(BF16)
    padded[SIDE : SIDE + CELLS, C : 2 * C] = hidden.astype(BF16)
    padded[SIDE : SIDE + CELLS, 2 * C : 3 * C] = shift_left(hidden, column).astype(BF16)


def norm_hidden(values, mask, temb, entries, matrix):
    mean = group_sums([col_sum(values * mask)], matrix)[0] / entries
    centered = values - mean
    variance = group_sums([col_sum(centered * centered * mask)], matrix)[0] / entries
    scale = lax.rsqrt(variance + 1e-05)
    normed = centered * scale
    shifted = normed + temb
    hidden = shifted / (1.0 + jnp.exp(-shifted)) * mask
    return normed, scale, hidden


def conv(padded, kernel):
    total = None
    for row in range(3):
        part = jnp.dot(
            padded[row * SIDE : row * SIDE + CELLS, :], kernel[row], preferred_element_type=F32
        )
        total = part if total is None else total + part
    return total


def conv_back(cot_padded, kernel, column):
    total = None
    for row in range(3):
        part = lax.dot_general(
            cot_padded[(2 - row) * SIDE : (2 - row) * SIDE + CELLS, :],
            kernel[row],
            NT,
            preferred_element_type=F32,
        )
        total = part if total is None else total + part
    left, middle, right = total[:, 0:C], total[:, C : 2 * C], total[:, 2 * C : 3 * C]
    return shift_left(left, column) + middle + shift_right(right, column)


def norm_back(hidden_cot, normed, scale, temb, mask, entries, matrix):
    shifted = normed + temb
    gate = 1.0 / (1.0 + jnp.exp(-shifted))
    flow = hidden_cot * mask * (gate * (1.0 + shifted * (1.0 - gate)))
    plain, cross = group_sums([col_sum(flow), col_sum(flow * normed)], matrix)
    return scale * (flow - mask * (plain / entries + normed * (cross / entries)))


def mask_of(bucket_ref, core):
    row = lax.broadcasted_iota(jnp.int32, (CELLS, C), 0)
    inside = (row // SIDE < bucket_ref[core, 0]) & (row % SIDE < bucket_ref[core, 1])
    return inside.astype(F32)


def entries_of(bucket_ref, core):
    return (bucket_ref[core, 0] * bucket_ref[core, 1] * (C // G)).astype(F32)


class Setup:
    def __init__(self, core, bucket, embedding, time_ref, matrix):
        self.core = core
        self.column = column_index()
        self.mask = mask_of(bucket, core)
        self.entries = entries_of(bucket, core)
        self.matrix = matrix[...]
        self.embedding = embedding
        self.time_ref = time_ref

    def temb(self, k, side):
        rows = jnp.dot(self.embedding[...], self.time_ref[k, side], preferred_element_type=F32)
        at = lax.broadcasted_iota(jnp.int32, rows.shape, 0)
        return col_sum(jnp.where(at == self.core, rows, 0.0))


def fetch_pair(core, own, other, target, sems):
    copies = [
        pltpu.make_async_copy(own, target.at[core], sems.at[0]),
        pltpu.make_async_copy(other, target.at[1 - core], sems.at[1]),
    ]
    for copy in copies:
        copy.start()
    return copies


def wait_all(*groups):
    for copies in groups:
        for copy in copies:
            copy.wait()


def forward_block(setup, values, k, side, kernel, padded, out):
    normed_ref, scale_ref, hidden_ref = out
    normed, scale, hidden = norm_hidden(
        values, setup.mask, setup.temb(k, side), setup.entries, setup.matrix
    )
    normed_ref[k] = normed
    scale_ref[k] = jnp.broadcast_to(scale, (8, C))
    hidden_ref[k] = hidden.astype(BF16)
    if kernel is None:
        return None
    store_windows(padded, hidden, setup.column)
    return ((values + conv(padded, kernel)) * setup.mask).astype(BF16)


def encoder_pair(setup, value, w_enc, padded, out, inputs_ref):
    for k in range(2):
        inputs_ref[k] = value
        value = forward_block(setup, value.astype(F32), k, 0, w_enc.at[k], padded, out)
    return value


def decoder_pair(setup, value, w_dec, padded, out, inputs_ref, last):
    for k in (1, 0):
        summed = value.astype(F32) + inputs_ref[k].astype(F32)
        kernel = w_dec.at[k] if last or k == 1 else None
        value = forward_block(setup, summed, k, 1, kernel, padded, out)
    return value


def backward_pair(setup, value, side, order, kernels, padded_cot, kept, cot_ref, skips, skip_in, last):
    normed_ref, scale_ref = kept
    for at, k in enumerate(order):
        residual = value.astype(F32) * setup.mask
        conv_cot = residual.astype(BF16)
        cot_ref[k] = conv_cot
        if at == 1 and not last:
            return None
        padded_cot[SIDE : SIDE + CELLS, :] = conv_cot
        hidden_cot = conv_back(padded_cot, kernels.at[k], setup.column)
        total = residual + norm_back(
            hidden_cot, normed_ref[k], scale_ref[k, 0:1], setup.temb(k, side), setup.mask,
            setup.entries, setup.matrix,
        )
        if skip_in is not None:
            total = total + skip_in[k].astype(F32)
        value = total.astype(BF16)
        if skips is not None:
            skips[k] = value
    return value


def phase_one(
    where, bucket, latents, time_own, time_other, enc_own, enc_other, emb, matrix,
    normed, scale, hidden, kept, sent, x, time_ref, w_enc, padded, sems,
):
    core = where[1]
    enc_copies = fetch_pair(core, enc_own, enc_other, w_enc, sems.at[0])
    time_copies = fetch_pair(core, time_own, time_other, time_ref, sems.at[1])
    x_copy = pltpu.make_async_copy(latents.at[core], x, sems.at[2, 0])
    x_copy.start()
    clear_edges(padded)
    wait_all([x_copy], time_copies, enc_copies)
    setup = Setup(core, bucket, emb, time_ref, matrix)
    sent[...] = encoder_pair(setup, x[...], w_enc, padded, (normed, scale, hidden), kept)


def phase_two(
    where, bucket, x, time_own, time_other, enc_own, enc_other, dec_own, dec_other, emb, matrix,
    e_normed, e_scale, e_hidden, d_normed, d_scale, d_hidden, sent,
    kept, time_ref, w_enc, w_dec, padded, sems,
):
    core = where[1]
    time_copies = fetch_pair(core, time_own, time_other, time_ref, sems.at[1])
    enc_copies = fetch_pair(core, enc_own, enc_other, w_enc, sems.at[0])
    dec_copies = fetch_pair(core, dec_own, dec_other, w_dec, sems.at[2])
    clear_edges(padded)
    wait_all(time_copies, enc_copies)
    setup = Setup(core, bucket, emb, time_ref, matrix)
    upper = encoder_pair(setup, x[...], w_enc, padded, (e_normed, e_scale, e_hidden), kept)
    wait_all(dec_copies)
    sent[...] = decoder_pair(
        setup, upper, w_dec, padded, (d_normed, d_scale, d_hidden), kept, True
    )


def phase_three(
    scaling, where, bucket, x, cotangent, time_own, time_other, dec_own, dec_other, kept, emb,
    matrix, d_hidden, cots, skips, sent,
    d_normed, d_scale, start, time_ref, w_dec, padded, padded_cot, sems,
):
    core = where[1]
    time_copies = fetch_pair(core, time_own, time_other, time_ref, sems.at[1])
    dec_copies = fetch_pair(core, dec_own, dec_other, w_dec, sems.at[0])
    start_copy = pltpu.make_async_copy(cotangent.at[core], start, sems.at[2, 0])
    start_copy.start()
    clear_edges(padded)
    clear_edges(padded_cot)
    wait_all(time_copies, dec_copies, [start_copy])
    setup = Setup(core, bucket, emb, time_ref, matrix)
    decoder_pair(setup, x[...], w_dec, padded, (d_normed, d_scale, d_hidden), kept, False)
    cot = (start[...].astype(F32) * scaling).astype(BF16)
    sent[...] = backward_pair(
        setup, cot, 1, (0, 1), w_dec, padded_cot, (d_normed, d_scale), cots, skips, None, True
    )


def phase_four(
    where, bucket, x, time_own, time_other, enc_own, enc_other, dec_own, dec_other, emb, matrix,
    d_normed, d_scale, e_normed, e_scale, d_cots, e_cots, sent,
    skips, time_ref, w_enc, w_dec, padded_cot, sems,
):
    core = where[1]
    time_copies = fetch_pair(core, time_own, time_other, time_ref, sems.at[1])
    dec_copies = fetch_pair(core, dec_own, dec_other, w_dec, sems.at[0])
    enc_copies = fetch_pair(core, enc_own, enc_other, w_enc, sems.at[2])
    clear_edges(padded_cot)
    wait_all(time_copies, dec_copies)
    setup = Setup(core, bucket, emb, time_ref, matrix)
    cot = backward_pair(
        setup, x[...], 1, (0, 1), w_dec, padded_cot, (d_normed, d_scale), d_cots, skips, None, True
    )
    wait_all(enc_copies)
    sent[...] = backward_pair(
        setup, cot, 0, (1, 0), w_enc, padded_cot, (e_normed, e_scale), e_cots, None, skips, True
    )


def store_packed(target, row, values):
    values = values.astype(target.dtype)
    first = row * TAPS
    target[first : first + TAPS, :] = values[:, 0:LANES]
    target[FLAT + first : FLAT + first + TAPS, :] = values[:, LANES : 2 * LANES]
    half = FLAT // 2
    for begin, end in ((0, TAPS), (0, TAPS // 2), (TAPS // 2, TAPS)):
        low, high = first + begin, first + end
        if row == 1 and end - begin == TAPS or row != 1 and end - begin != TAPS:
            continue
        side = 0 if high <= half else 1
        at = 2 * FLAT + low - side * half
        target[at : at + end - begin, side * TAIL : (side + 1) * TAIL] = values[
            begin:end, 2 * LANES : C
        ]


def store_gradients(core, hidden, cots, own, other, padded_cot, turned):
    column = column_index()
    own[PACKED_USED:, :] = jnp.zeros((PACKED - PACKED_USED, LANES), F32)
    other[PACKED_USED:, :] = jnp.zeros((PACKED - PACKED_USED, LANES), BF16)
    for k in range(2):
        values = hidden[k].astype(F32)
        padded_cot[SIDE : SIDE + CELLS, :] = cots[k]
        turned[0:C, :] = shift_right(values, column).T.astype(BF16)
        turned[C : 2 * C, :] = values.T.astype(BF16)
        turned[2 * C : 3 * C, :] = shift_left(values, column).T.astype(BF16)
        for row in range(3):
            part = jnp.dot(
                turned[...],
                padded_cot[(2 - row) * SIDE : (2 - row) * SIDE + CELLS, :],
                preferred_element_type=F32,
            )

            @pl.when(core == k)
            def _(part=part, row=row):
                store_packed(own, row, part)

            @pl.when(core != k)
            def _(part=part, row=row):
                store_packed(other, row, part)


def weight_phase(
    where, a_hidden, a_cots, b_hidden, b_cots, own, other, padded_cot, turned, hidden, cots
):
    clear_edges(padded_cot)

    @pl.when(where[0] == 0)
    def _():
        hidden[...] = a_hidden[...]
        cots[...] = a_cots[...]

    @pl.when(where[0] != 0)
    def _():
        hidden[...] = b_hidden[...]
        cots[...] = b_cots[...]

    store_gradients(where[1], hidden, cots, own, other, padded_cot, turned)


def phase_five(
    where, bucket, x, time_own, time_other, enc_own, enc_other, skips, emb, matrix,
    e_normed, e_scale, a_hidden, b_hidden, b_cots,
    own, other, padded_cot, turned, hidden, cots, time_ref, w_enc, sems,
):
    clear_edges(padded_cot)
    core = where[1]
    time_copies = fetch_pair(core, time_own, time_other, time_ref, sems.at[1])
    enc_copies = fetch_pair(core, enc_own, enc_other, w_enc, sems.at[0])
    wait_all(time_copies, enc_copies)

    @pl.when(where[0] == 0)
    def _():
        hidden[...] = a_hidden[...]
        setup = Setup(core, bucket, emb, time_ref, matrix)
        backward_pair(
            setup, x[...], 0, (1, 0), w_enc, padded_cot, (e_normed, e_scale), cots, None, skips,
            False,
        )

    @pl.when(where[0] != 0)
    def _():
        hidden[...] = b_hidden[...]
        cots[...] = b_cots[...]

    store_gradients(core, hidden, cots, own, other, padded_cot, turned)


def unpack(packed, grad):
    half = FLAT // 2
    grad[:, 0:LANES] = packed[0:FLAT, :].astype(F32)
    grad[:, LANES : 2 * LANES] = packed[FLAT : 2 * FLAT, :].astype(F32)
    tail = packed[2 * FLAT : PACKED_USED, :].astype(F32)
    grad[0:half, 2 * LANES : C] = tail[:, 0:TAIL]
    grad[half:FLAT, 2 * LANES : C] = tail[:, TAIL : 2 * TAIL]


def shape(dims, dtype):
    return jax.ShapeDtypeStruct(dims, dtype)


NORMED = ((2, CELLS, C), F32)
SCALE = ((2, 8, C), F32)
ACTS = ((2, CELLS, C), BF16)
ONE = ((CELLS, C), BF16)
PADDED = pltpu.VMEM((CELLS + 2 * SIDE, TAPS), BF16)
PADDED_COT = pltpu.VMEM((CELLS + 2 * SIDE, C), BF16)
TURNED = pltpu.VMEM((TAPS, CELLS), BF16)
OWN = ((PACKED, LANES), F32)
OTHER = ((PACKED, LANES), BF16)
WEIGHTS = pltpu.VMEM((2, 3, TAPS, C), BF16)
TIMES = pltpu.VMEM((2, 2, C, C), BF16)
SEMS = pltpu.SemaphoreType.DMA((3, 2))


def call(body, spaces, outs, scratch, flops, name):
    def run(*args):
        kinds = {"s": pltpu.SMEM, "h": pl.ANY, "v": pltpu.VMEM}
        moved = sum(a.size * a.dtype.itemsize for a in args) + sum(
            math.prod(d) * jnp.dtype(t).itemsize for d, t in outs
        )
        return pl.pallas_call(
            body,
            out_shape=tuple(shape(d, t) for d, t in outs),
            in_specs=[pl.BlockSpec(memory_space=kinds[space]) for space in spaces],
            out_specs=tuple(pl.BlockSpec(memory_space=pltpu.VMEM) for _ in outs),
            scratch_shapes=list(scratch),
            compiler_params=pltpu.CompilerParams(vmem_limit_bytes=VMEM_LIMIT),
            cost_estimate=pl.CostEstimate(flops=flops, bytes_accessed=moved, transcendentals=0),
            name=name,
        )(*args)

    return run


CONV = 2 * CELLS * 9 * C * C


def time_embed(timesteps):
    half_width = C // 2
    frequencies = jnp.exp(
        -math.log(10000.0) * jnp.arange(half_width, dtype=F32) / half_width
    )
    angles = timesteps.astype(F32)[:, None] * frequencies[None, :]
    return jnp.concatenate([jnp.cos(angles), jnp.sin(angles)], axis=1).astype(BF16)


DP = ("z", "far", "y")


def row_major(array):
    return with_layout_constraint(array, Layout(major_to_minor=tuple(range(array.ndim))))


def to_other_core(array):
    swap = [(0, 1), (1, 0)]
    return row_major(lax.ppermute(row_major(array), "core", swap))


def sum_by_scatter(pair):
    part = lax.psum_scatter(pair.astype(BF16), DP, scatter_dimension=0, tiled=True)
    return lax.all_gather(part, DP, axis=0, tiled=True)


def sum_by_exchange(pair):
    count = lax.axis_size(DP)
    parts = lax.all_to_all(
        pair.astype(BF16).reshape(count, -1, LANES), DP, split_axis=0, concat_axis=0, tiled=True
    )
    part = jnp.sum(parts.astype(F32), axis=0).astype(BF16)
    return lax.all_gather(part, DP, axis=0, tiled=True)


def local(latents, cotangent, bucket, timesteps, w_enc, w_dec, w_time):
    where = jnp.stack([lax.axis_index("near"), lax.axis_index("core")]).astype(jnp.int32)
    micro_count = latents.shape[0]
    loss_scale = float(micro_count * lax.axis_size(DP) * CELLS) ** (-0.5)

    enc = w_enc.reshape(3, TAPS, C)
    dec = w_dec.reshape(3, TAPS, C)
    times = w_time.reshape(2, C, C)
    enc = (enc, to_other_core(enc))
    times = (times, to_other_core(times))
    dec = (dec, to_other_core(dec))
    latents = latents.reshape(micro_count, CELLS, C)
    cotangent = cotangent.reshape(micro_count, CELLS, C)
    emb = jnp.pad(time_embed(timesteps), ((0, 16 - micro_count), (0, 0)))
    matrix = group_matrix()

    def up(value):
        return lax.ppermute(value, "near", [(0, 1)])

    def down(value):
        return lax.ppermute(value, "near", [(1, 0)])

    one = call(
        phase_one, "ss" + "h" * 5 + "vv", [NORMED, SCALE, ACTS, ACTS, ONE],
        [pltpu.VMEM(*ONE), TIMES, WEIGHTS, PADDED, SEMS], 2 * CONV, "one",
    )
    a_normed, a_scale, a_hidden, a_kept, sent = one(
        where, bucket, latents, *times, *enc, emb, matrix
    )
    two = call(
        phase_two, "ssv" + "h" * 6 + "vv", [NORMED, SCALE, ACTS, NORMED, SCALE, ACTS, ONE],
        [pltpu.VMEM(*ACTS), TIMES, WEIGHTS, WEIGHTS, PADDED, SEMS], 4 * CONV, "two",
    )
    be_normed, be_scale, be_hidden, bd_normed, bd_scale, bd_hidden, sent = two(
        where, bucket, up(sent), *times, *enc, *dec, emb, matrix
    )
    three = call(
        functools.partial(phase_three, loss_scale), "ssv" + "h" * 5 + "vvv",
        [ACTS, ACTS, ACTS, ONE],
        [
            pltpu.VMEM(*NORMED), pltpu.VMEM(*SCALE), pltpu.VMEM(*ONE), TIMES, WEIGHTS, PADDED,
            PADDED_COT, SEMS,
        ],
        3 * CONV, "three",
    )
    ad_hidden, ad_cots, a_skips, sent = three(
        where, bucket, down(sent), cotangent, *times, *dec, a_kept, emb, matrix
    )
    four = call(
        phase_four, "ssv" + "h" * 6 + "v" * 6, [ACTS, ACTS, ONE],
        [pltpu.VMEM(*ACTS), TIMES, WEIGHTS, WEIGHTS, PADDED_COT, SEMS], 4 * CONV, "four",
    )
    bd_cots, be_cots, sent = four(
        where, bucket, up(sent), *times, *enc, *dec, emb, matrix,
        bd_normed, bd_scale, be_normed, be_scale,
    )
    received = down(sent)
    work = [PADDED_COT, TURNED, pltpu.VMEM(*ACTS), pltpu.VMEM(*ACTS)]
    weights = call(weight_phase, "svvvv", [OWN, OTHER], work, 2 * CONV, "weights")
    own_dec, other_dec = weights(where, ad_hidden, ad_cots, bd_hidden, bd_cots)
    five = call(
        phase_five, "ssv" + "h" * 4 + "v" * 8, [OWN, OTHER], [*work, TIMES, WEIGHTS, SEMS],
        3 * CONV, "five",
    )
    own_enc, other_enc = five(
        where, bucket, received, *times, *enc, a_skips, emb, matrix, a_normed, a_scale, a_hidden,
        be_hidden, be_cots,
    )
    spread = call(unpack, "v", [((FLAT, C), F32)], [], 0, "unpack")

    def finish(own, other, add):
        pair = own + lax.ppermute(other, "core", [(0, 1), (1, 0)]).astype(F32)
        (grad,) = spread(add(pair))
        return grad.reshape(1, 3, 3, C, C)

    grad_dec = finish(own_dec, other_dec, sum_by_scatter)
    return finish(own_enc, other_enc, sum_by_exchange), grad_dec


def solution(mesh):
    segments, dp = mesh.shape["segment"], mesh.shape["dp"]
    near, far, rows = segments // 2, 2, 4
    split = Mesh(
        mesh.devices.reshape(near, 2, dp // (far * rows), far, rows),
        ("near", "core", "z", "far", "y"),
    )
    section, micro = ("near", "core"), ("z", "far", "y")
    placed = (
        P(micro, None, None, None),
        P(micro, None, None, None),
        P(micro, None),
        P(micro),
        P(section, None, None, None, None),
        P(section, None, None, None, None),
        P(section, None, None, None),
    )
    grads = P(section, None, None, None, None)
    return jax.shard_map(
        local, mesh=split, in_specs=placed, out_specs=(grads, grads), check_vma=False
    )
```

time: 1150 us -> 720 us (0.63)
  waiting for transfers between devices: 774 us -> 595 us
  matrix products: 131 us -> 0 us
  other arithmetic: 110 us -> 4.8 us
  Pallas kernels: 0 us -> 47.5 us
  starting transfers between devices: 48.3 us -> 20.8 us
  loops' own time: 16.9 us -> 0 us
  local copies, waits for them, and re-layouts: 51.4 us -> 35.3 us
    psum x1 -> x0, waiting for transfers between devices: 733 us -> none  [local(): summed_enc, summed_dec = lax.psum((grad_enc, grad_dec), 'dp')]
    reduce_scatter x0 -> x1, waiting for transfers between devices: none -> 339 us  [sum_by_scatter(): lax.psum_scatter(pair.astype(BF16), DP, scatter_dimension=0, tiled=True)]
    all_gather x0 -> x2, waiting for transfers between devices: none -> 234 us  [the longest x1 117 us: sum_by_scatter(): return lax.all_gather(part, DP, axis=0, tiled=True)]
    dot_general x92 -> x0, matrix products: 78.2 us -> none  [the longest x90 75.9 us: weight_grad(): lax.dot_general(window, flat_cot, (((0,), (0,)), ((), ())), preferred_ele...]
    conv_general_dilated x20 -> x0, matrix products: 53.3 us -> none  [conv_apply(): lax.conv_general_dilated(hidden, kernel, (1, 1), 'SAME', dimension_number...]
    pallas_call x0 -> x8, Pallas kernels: none -> 47.5 us  [run(): pl.pallas_call(body, out_shape=tuple((shape(d, t) for d, t in outs)), in_...]
    add x10 -> x0, other arithmetic: 45.8 us -> none  [the longest x5 22.9 us: dec_back_tick(): accum + jnp.where(active, weight_grad(item(dec_hidden, slot), cot_conv),...]
    ppermute x20 -> x9, starting transfers between devices: 48.2 us -> 7.05 us  [the longest x2 3.78 us: down(): return lax.ppermute(value, 'near', [(1, 0)])]
  transfers between devices with their start and end apart: 21 -> 13, of which waited for: 11 -> 10; matrix products, arithmetic and copies ran while one was open for 12% -> 2% of each run, Pallas kernels for 0% -> 2%
where the time goes in v1:
time: 720 us; the launch traced here: 718 us
  waiting for transfers between devices  595 us (83%)
  Pallas kernels  47.5 us (7%)
  local copies, waits for them, and re-layouts  35.3 us (5%)
  starting transfers between devices  20.8 us (3%)
  between operations  14 us (2%)
    reduce_scatter x1, waiting for transfers between devices, sum_by_scatter(): lax.psum_scatter(pair.astype(BF16), DP, scatter_dimension=0, tiled=True)  339 us
    all_gather x1, waiting for transfers between devices, sum_by_scatter(): return lax.all_gather(part, DP, axis=0, tiled=True)  117 us
    all_gather x1, waiting for transfers between devices, sum_by_exchange(): return lax.all_gather(part, DP, axis=0, tiled=True)  116 us
    pallas_call x8, Pallas kernels, run(): pl.pallas_call(body, out_shape=tuple((shape(d, t) for d, t in outs)), in_...  47.5 us
    unnamed x60, local copies, waits for them, and re-layouts  20.6 us
  transfers between devices with their start and end apart: 13, of which 10 were waited for; matrix products, arithmetic and copies ran while one was open for 2% of the time, Pallas kernels for 2%

profile of v1, /device:TPU:2, one launch (start us, length us, event | category | flops | bytes accessed | tf_op | source)
XLA Modules:
  0.0 717.7 jit_solution(18116911221275720300)
XLA Ops:
  7.2 4.2 copy.10
  11.5 2.4 copy.12
  15.7 4.1 copy.11.enc_other
  19.9 1.6 copy-done.1
  22.5 6.0 one.1
  32.2 4.1 copy.13.dec_other
  36.3 3.8 collective-permute-done.2.x
  40.0 1.6 copy-done.2
  41.7 1.6 copy-done.6
  43.3 1.6 copy-done.8
  44.9 9.4 %two.1 = (f32[2,256,320]{2,1,0:T(8,128)S(1)}, f32[2,8,320]{2,1,0:T(8,128)S(1)}, bf16[2,256,320]{2,1,0:T(8,128)(2,1)S(1)}, f32[2,256,320]{2,1,0:T(8,128)S(1)}, f3...) custom-call(s32[2]{0:T(128)S(1)} %pad_add_fusion.where, ...), custom_call_target="tpu_custom_call" | custom-call | flops 1887436800 | bytes 10741784 | tf_op jit(solution)/shard_map/two/pallas_call | solution.py:414
  54.3 1.6 collective-permute-start.4
  56.0 4.0 collective-permute-done.4.x
  60.0 7.4 %three.1 = (bf16[2,256,320]{2,1,0:T(8,128)(2,1)S(1)}, bf16[2,256,320]{2,1,0:T(8,128)(2,1)S(1)}, bf16[2,256,320]{2,1,0:T(8,128)(2,1)S(1)}, bf16[256,320]{1,0:T(8,128)(2,1)S(1)}) custom-call(s32[2]{0:T(128)S(1)} %pad_add_fusion.where, s32[2,2]{1,0:T(2,128)S(1)} %copy-done.28, bf16[256,320]{1,0:T(8,128)(2,1)S(1)} %collective-permute-done.4.x, ...), custom_call_target="tpu_custom_call" | custom-call | flops 1415577600 | bytes 6686744 | tf_op jit(solution)/shard_map/three/pallas_call | solution.py:414
  68.7 6.5 collective-permute-done.5.x
  75.2 9.4 %four.1 = (bf16[2,256,320]{2,1,0:T(8,128)(2,1)S(1)}, bf16[2,256,320]{2,1,0:T(8,128)(2,1)S(1)}, bf16[256,320]{1,0:T(8,128)(2,1)}) custom-call(s32[2]{0:T(128)S(1)} %pad_add_fusion.where, s32[2,2]{1,0:T(2,128)S(1)} %copy-done.28, bf16[256,320]{1,0:T(8,128)(2,1)S(1)} %collective-permute-done.5.x, bf16[2,320,320]{2,1,0:T(8,128)(2,1)S(1)} %bitcast.23, ...), custom_call_target="tpu_custom_call" | custom-call | flops 1887436800 | bytes 10741784 | tf_op jit(solution)/shard_map/four/pallas_call | solution.py:414
  85.4 4.5 weights.1
  90.0 2.1 collective-permute-start.6
  92.1 2.0 collective-permute-done.8
  94.1 1.7 add_convert_fusion
  96.6 1.6 copy-done.4
  103.4 6.0 five.1
  109.5 4.1 collective-permute-done.7
  113.6 1.9 add_convert_fusion.1
  115.5 13.7 %all-to-all-start = ((bf16[64,128,128]{2,1,0:T(8,128)(2,1)}), bf16[64,128,128]{2,1,0:T(8,128)(2,1)S(1)}, u32[]{:S(2)}, u32[]{:S(2)}) async-start(bf16[64,128,128]{2,1,0:T(8,128)(2,1)} %bitcast.27), calls=%async_computation | async-start | bytes 4194304 | tf_op jit(solution)/shard_map/all_to_all | solution.py:459
  129.2 339.4 %reduce-scatter.2.cloned.1.call-done = bf16[128,128]{1,0:T(8,128)(2,1)} async-done(((bf16[8192,128]{1,0:T(8,128)(2,1)}), bf16[128,128]{1,0:T(8,128)(2,1)}) %reduce-scatter.2.cloned.1.call-update) | async-done | bytes 32784 | tf_op jit(solution)/shard_map/reduce_scatter | solution.py:453
  469.6 117.4 %all-gather.5.cloned.1.call-done.packed = bf16[8192,128]{1,0:T(8,128)(2,1)} async-done(((bf16[128,128]{1,0:T(8,128)(2,1)}), bf16[8192,128]{1,0:T(8,128)(2,1)}) %all-gather.5.cloned.1.call-update) | async-done | bytes 2097168 | tf_op jit(solution)/shard_map/all_gather | solution.py:454
  587.0 1.6 copy-done.12
  588.6 2.4 unpack.3
  591.0 116.1 %all-gather.3.cloned.1.call-done.packed = bf16[8192,128]{1,0:T(8,128)(2,1)} async-done(((bf16[128,128]{1,0:T(8,128)(2,1)}), bf16[8192,128]{1,0:T(8,128)(2,1)}) %all-gather.3.cloned.1.call-update) | async-done | bytes 2097168 | tf_op jit(solution)/shard_map/all_gather | solution.py:463
  707.2 1.6 copy-done.13
  708.8 2.4 unpack.2
  (77 shorter events, 15.9 us)
Async XLA Ops:
  7.2 4.3 copy-start.5
  7.2 461.4 %reduce-scatter.2.cloned.1.call-start = ((), (), s32[]{:S(2)}) async-start(), calls=%async_computation.3 | async-start | bytes 2129920 | tf_op jit(solution)/shard_map/reduce_scatter | solution.py:453
  11.4 2.9 copy-start.10
  11.4 4.3 collective-permute-start.1
  11.4 2.9 copy-start.29
  13.8 18.4 %collective-permute-start.3 = (bf16[3,960,320]{1,2,0:T(8,128)(2,1)}, bf16[3,960,320]{1,2,0:T(8,128)(2,1)}, u32[]{:S(2)}, u32[]{:S(2)}) collective-permute-start(bf16[3,960,320]{1,2,0:T(8,128)(2,1)} %copy.12), channel_id=1, source_target_pairs={{0,64},{64,0},{1,65},{65,1},{2,66},{66,2},{3,67},{67,3},{4,68},{68... | collective-permute-start | bytes 5529608 | tf_op jit(solution)/shard_map/ppermute | solution.py:449
  14.3 5.5 collective-permute-start
  14.5 5.3 copy-start
  14.6 5.3 copy-start.11
  14.6 5.3 copy-start.28
  19.8 1.6 copy-start.1
  30.9 9.1 %collective-permute-start.2 = (bf16[256,320]{1,0:T(8,128)(2,1)}, bf16[256,320]{1,0:T(8,128)(2,1)}, u32[]{:S(2)}, u32[]{:S(2)}) collective-permute-start(bf16[256,320]{1,0:T(8,128)(2,1)} %get-tuple-element.25), channel_id=1, source_target_pairs={{0,128},{1,129},{2,130},{3,131},{4,132},{5,133},{6,134},{7,135},{8... | collective-permute-start | bytes 491528 | tf_op jit(solution)/shard_map/ppermute | solution.py:483
  40.0 1.6 copy-start.2
  41.7 1.6 copy-start.6
  43.3 1.6 copy-start.8
  44.9 15.1 %copy-start.7 = (bf16[1,3,3,320,320]{4,3,2,1,0:T(8,128)(2,1)S(1)}, bf16[1,3,3,320,320]{4,3,2,1,0:T(8,128)(2,1)}, u32[]{:S(2)}) copy-start(bf16[1,3,3,320,320]{4,3,2,1,0:T(8,128)(2,1)} %param.13) | copy-start | bytes 5529604
  44.9 15.1 %copy-start.9 = (bf16[3,960,320]{2,1,0:T(8,128)(2,1)S(1)}, bf16[3,960,320]{2,1,0:T(8,128)(2,1)}, u32[]{:S(2)}) copy-start(bf16[3,960,320]{2,1,0:T(8,128)(2,1)} %copy.13.dec_other) | copy-start | bytes 5529604
  44.9 15.1 %copy-start.25 = (bf16[2,16,16,320]{3,2,1,0:T(8,128)(2,1)S(1)}, bf16[2,16,16,320]{3,2,1,0:T(8,128)(2,1)}, u32[]{:S(2)}) copy-start(bf16[2,16,16,320]{3,2,1,0:T(8,128)(2,1)} %param.9) | copy-start | bytes 983044
  44.9 15.1 %copy-start.27 = (bf16[2,256,320]{2,1,0:T(8,128)(2,1)S(1)}, bf16[2,256,320]{2,1,0:T(8,128)(2,1)}, u32[]{:S(2)}) copy-start(bf16[2,256,320]{2,1,0:T(8,128)(2,1)} %copy-done.26) | copy-start | bytes 983044
  54.3 13.1 %copy-start.18 = (bf16[2,256,320]{2,1,0:T(8,128)(2,1)}, bf16[2,256,320]{2,1,0:T(8,128)(2,1)S(1)}, u32[]{:S(2)}) copy-start(bf16[2,256,320]{2,1,0:T(8,128)(2,1)S(1)} %get-tuple-element.38.b_hidden) | copy-start | bytes 983044
  54.3 5.6 collective-permute-start.4
  60.0 15.3 %copy-start.3 = (bf16[3,960,320]{2,1,0:T(8,128)(2,1)S(1)}, bf16[3,960,320]{2,1,0:T(8,128)(2,1)}, u32[]{:S(2)}) copy-start(bf16[3,960,320]{2,1,0:T(8,128)(2,1)} %copy.11.enc_other) | copy-start | bytes 5529604
  67.4 17.2 %copy-start.20 = (bf16[2,256,320]{2,1,0:T(8,128)(2,1)}, bf16[2,256,320]{2,1,0:T(8,128)(2,1)S(1)}, u32[]{:S(2)}) copy-start(bf16[2,256,320]{2,1,0:T(8,128)(2,1)S(1)} %get-tuple-element.34.skips) | copy-start | bytes 983044
  67.4 7.8 %collective-permute-start.5 = (bf16[256,320]{1,0:T(8,128)(2,1)S(1)}, bf16[256,320]{1,0:T(8,128)(2,1)S(1)}, u32[]{:S(2)}, u32[]{:S(2)}) collective-permute-start(bf16[256,320]{1,0:T(8,128)(2,1)S(1)} %get-tuple-element.28), channel_id=1, source_target_pairs={{0,128},{1,129},{2,130},{3,131},{4,132},{5,133},{6,134},{7,135},{8... | collective-permute-start | bytes 491528 | tf_op jit(solution)/shard_map/ppermute | solution.py:483
  89.9 4.2 collective-permute-start.8
  90.0 6.7 collective-permute-start.6
  96.6 1.6 copy-start.4
  109.4 4.2 collective-permute-start.7
  115.5 353.2 %all-to-all-start = ((bf16[64,128,128]{2,1,0:T(8,128)(2,1)}), bf16[64,128,128]{2,1,0:T(8,128)(2,1)S(1)}, u32[]{:S(2)}, u32[]{:S(2)}) async-start(bf16[64,128,128]{2,1,0:T(8,128)(2,1)} %bitcast.27), calls=%async_computation | async-start | bytes 4194304 | tf_op jit(solution)/shard_map/all_to_all | solution.py:459
  129.2 457.9 %all-gather.5.cloned.1.call-start = ((), (), s32[]{:S(2)}) async-start(), calls=%async_computation.4 | async-start | bytes 2129920 | tf_op jit(solution)/shard_map/all_gather | solution.py:454
  468.6 238.5 %all-gather.3.cloned.1.call-start = ((), (), s32[]{:S(2)}) async-start(), calls=%async_computation.2 | async-start | bytes 2129920 | tf_op jit(solution)/shard_map/all_gather | solution.py:463
  587.0 1.6 copy-start.12
  (11 other events, 10.9 us)
Sparse Core Ops, SparseCore 0:
  96.0 372.5 reduce-scatter.1
  472.7 114.2 all-gather.4
  591.8 115.3 all-gather.2

commit v2 on v1

--- a/solution.py
+++ b/solution.py
@@ -6,7 +6,6 @@
 import numpy as np
 from jax import lax
 from jax.experimental import pallas as pl
-from jax.experimental.layout import Layout, with_layout_constraint
 from jax.experimental.pallas import tpu as pltpu
 from jax.sharding import Mesh, PartitionSpec as P
 
@@ -17,12 +16,12 @@
 TAPS = 3 * C
 F32 = jnp.float32
 BF16 = jnp.bfloat16
-VMEM_LIMIT = 40 * 1024 * 1024
+VMEM_LIMIT = 30 * 1024 * 1024
 LANES = 128
 FLAT = 9 * C
 TAIL = C - 2 * LANES
 PACKED_USED = 2 * FLAT + FLAT // 2
-PACKED = 64 * 128
+PACKED = 64 * 120
 
 NT = (((1,), (1,)), ((), ()))
 
@@ -88,11 +87,15 @@
     return normed, scale, hidden
 
 
+def taps(kernel, row):
+    return kernel[3 * row : 3 * row + 3].reshape(TAPS, C)
+
+
 def conv(padded, kernel):
     total = None
     for row in range(3):
         part = jnp.dot(
-            padded[row * SIDE : row * SIDE + CELLS, :], kernel[row], preferred_element_type=F32
+            padded[row * SIDE : row * SIDE + CELLS, :], taps(kernel, row), preferred_element_type=F32
         )
         total = part if total is None else total + part
     return total
@@ -103,7 +106,7 @@
     for row in range(3):
         part = lax.dot_general(
             cot_padded[(2 - row) * SIDE : (2 - row) * SIDE + CELLS, :],
-            kernel[row],
+            taps(kernel, row),
             NT,
             preferred_element_type=F32,
         )
@@ -400,14 +403,14 @@
 TURNED = pltpu.VMEM((TAPS, CELLS), BF16)
 OWN = ((PACKED, LANES), F32)
 OTHER = ((PACKED, LANES), BF16)
-WEIGHTS = pltpu.VMEM((2, 3, TAPS, C), BF16)
+WEIGHTS = pltpu.VMEM((2, 9, C, C), BF16)
 TIMES = pltpu.VMEM((2, 2, C, C), BF16)
 SEMS = pltpu.SemaphoreType.DMA((3, 2))
 
 
 def call(body, spaces, outs, scratch, flops, name):
     def run(*args):
-        kinds = {"s": pltpu.SMEM, "h": pl.ANY, "v": pltpu.VMEM}
+        kinds = {"s": pltpu.SMEM, "h": pltpu.HBM, "v": pltpu.VMEM}
         moved = sum(a.size * a.dtype.itemsize for a in args) + sum(
             math.prod(d) * jnp.dtype(t).itemsize for d, t in outs
         )
@@ -440,27 +443,27 @@
 DP = ("z", "far", "y")
 
 
-def row_major(array):
-    return with_layout_constraint(array, Layout(major_to_minor=tuple(range(array.ndim))))
-
-
 def to_other_core(array):
-    swap = [(0, 1), (1, 0)]
-    return row_major(lax.ppermute(row_major(array), "core", swap))
-
-
-def sum_by_scatter(pair):
-    part = lax.psum_scatter(pair.astype(BF16), DP, scatter_dimension=0, tiled=True)
-    return lax.all_gather(part, DP, axis=0, tiled=True)
-
-
-def sum_by_exchange(pair):
-    count = lax.axis_size(DP)
+    return lax.ppermute(array, "core", [(0, 1), (1, 0)])
+
+
+def scatter_sum(rows, axes):
+    count = lax.axis_size(axes)
     parts = lax.all_to_all(
-        pair.astype(BF16).reshape(count, -1, LANES), DP, split_axis=0, concat_axis=0, tiled=True
-    )
-    part = jnp.sum(parts.astype(F32), axis=0).astype(BF16)
-    return lax.all_gather(part, DP, axis=0, tiled=True)
+        rows.astype(BF16).reshape(count, -1, LANES), axes, split_axis=0, concat_axis=0, tiled=True
+    )
+    return jnp.sum(parts.astype(F32), axis=0)
+
+
+def gather_rows(rows, axes):
+    count = lax.axis_size(axes)
+    spread = jnp.broadcast_to(rows[None], (count, *rows.shape))
+    return lax.all_to_all(spread, axes, split_axis=0, concat_axis=0, tiled=True).reshape(-1, LANES)
+
+
+def sum_over_dp(pair):
+    part = scatter_sum(scatter_sum(pair, "y"), ("z", "far")).astype(BF16)
+    return gather_rows(gather_rows(part, ("z", "far")), "y")
 
 
 def local(latents, cotangent, bucket, timesteps, w_enc, w_dec, w_time):
@@ -468,8 +471,8 @@
     micro_count = latents.shape[0]
     loss_scale = float(micro_count * lax.axis_size(DP) * CELLS) ** (-0.5)
 
-    enc = w_enc.reshape(3, TAPS, C)
-    dec = w_dec.reshape(3, TAPS, C)
+    enc = w_enc.reshape(9, C, C)
+    dec = w_dec.reshape(9, C, C)
     times = w_time.reshape(2, C, C)
     enc = (enc, to_other_core(enc))
     times = (times, to_other_core(times))
@@ -533,13 +536,13 @@
     )
     spread = call(unpack, "v", [((FLAT, C), F32)], [], 0, "unpack")
 
-    def finish(own, other, add):
+    def finish(own, other):
         pair = own + lax.ppermute(other, "core", [(0, 1), (1, 0)]).astype(F32)
-        (grad,) = spread(add(pair))
+        (grad,) = spread(sum_over_dp(pair))
         return grad.reshape(1, 3, 3, C, C)
 
-    grad_dec = finish(own_dec, other_dec, sum_by_scatter)
-    return finish(own_enc, other_enc, sum_by_exchange), grad_dec
+    grad_dec = finish(own_dec, other_dec)
+    return finish(own_enc, other_enc), grad_dec
 
 
 def solution(mesh):

time: 720 us -> 282 us (0.39)
  waiting for transfers between devices: 595 us -> 130 us
  blocking collectives: 0 us -> 40.5 us
  local copies, waits for them, and re-layouts: 35.3 us -> 9.94 us
  starting transfers between devices: 20.8 us -> 36.5 us
  between operations: 14 us -> 0.88 us
    reduce_scatter x1 -> x0, waiting for transfers between devices: 339 us -> none  [sum_by_scatter(): lax.psum_scatter(pair.astype(BF16), DP, scatter_dimension=0, tiled=True)]
    all_gather x2 -> x0, waiting for transfers between devices: 234 us -> none  [the longest x1 117 us: sum_by_scatter(): return lax.all_gather(part, DP, axis=0, tiled=True)]
    all_to_all x1 -> x6, waiting for transfers between devices: 0.01 us -> 101 us  [the longest x4 71.7 us: scatter_sum(): lax.all_to_all(rows.astype(BF16).reshape(count, -1, LANES), axes, split_a...]
    all_to_all x0 -> x2, blocking collectives: none -> 40.5 us  [gather_rows(): lax.all_to_all(spread, axes, split_axis=0, concat_axis=0, tiled=True)]
    all_to_all x1 -> x6, starting transfers between devices: 13.7 us -> 29.8 us  [the longest x4 22.6 us: scatter_sum(): lax.all_to_all(rows.astype(BF16).reshape(count, -1, LANES), axes, split_a...]
    unnamed x60 -> x26, local copies, waits for them, and re-layouts: 20.6 us -> 7.26 us
    ppermute x2 -> x0, local copies, waits for them, and re-layouts: 8.15 us -> none  [to_other_core(): return row_major(lax.ppermute(row_major(array), 'core', swap))]
  transfers between devices with their start and end apart: 13 -> 15, of which waited for: 10 -> 11; matrix products, arithmetic and copies ran while one was open for 2% -> 4% of each run, Pallas kernels for 2% -> 5%
where the time goes in v2:
time: 282 us; the launch traced here: 277 us
  waiting for transfers between devices  130 us (46%)
  Pallas kernels  47.9 us (17%)
  blocking collectives  40.5 us (14%)
  starting transfers between devices  36.5 us (13%)
  other arithmetic  11.4 us (4%)
  local copies, waits for them, and re-layouts  9.94 us (4%)
    all_to_all x4, waiting for transfers between devices, scatter_sum(): lax.all_to_all(rows.astype(BF16).reshape(count, -1, LANES), axes, split_a...  71.7 us
    pallas_call x8, Pallas kernels, run(): pl.pallas_call(body, out_shape=tuple((shape(d, t) for d, t in outs)), in_...  47.9 us
    all_to_all x2, blocking collectives, gather_rows(): lax.all_to_all(spread, axes, split_axis=0, concat_axis=0, tiled=True)  40.5 us
    all_to_all x2, waiting for transfers between devices, gather_rows(): lax.all_to_all(spread, axes, split_axis=0, concat_axis=0, tiled=True)  29.6 us
    all_to_all x4, starting transfers between devices, scatter_sum(): lax.all_to_all(rows.astype(BF16).reshape(count, -1, LANES), axes, split_a...  22.6 us
    ppermute x2, waiting for transfers between devices, up(): return lax.ppermute(value, 'near', [(0, 1)])  13.8 us
    ppermute x2, waiting for transfers between devices, down(): return lax.ppermute(value, 'near', [(1, 0)])  8.45 us
    unnamed x26, local copies, waits for them, and re-layouts  7.26 us
  transfers between devices with their start and end apart: 15, of which 11 were waited for; matrix products, arithmetic and copies ran while one was open for 4% of the time, Pallas kernels for 5%

profile of v2, /device:TPU:2, one launch (start us, length us, event | category | flops | bytes accessed | tf_op | source)
XLA Modules:
  0.0 277.2 jit_solution(11369111314460752696)
XLA Ops:
  2.3 6.5 %collective-permute-done.time_other = bf16[2,320,320]{2,1,0:T(8,128)(2,1)S(1)} collective-permute-done((bf16[2,320,320]{2,1,0:T(8,128)(2,1)}, bf16[2,320,320]{2,1,0:T(8,128)(2,1)S(1)}, u32[]{:S(2)}, u32[]{:S(2)}) %collective-permute-start) | collective-permute-done | bytes 409632 | tf_op jit(solution)/shard_map/ppermute | solution.py:447
  8.8 1.6 copy-done
  14.1 5.3 %one.1 = (f32[2,256,320]{2,1,0:T(8,128)S(1)}, f32[2,8,320]{2,1,0:T(8,128)S(1)}, bf16[2,256,320]{2,1,0:T(8,128)(2,1)S(1)}, bf16[2,256,320]{2,1,0:T(8,128)(2,1)S(1)}, bf16[256,320]{1,0:T(8,128)(2,1)S(1)}) custom-call(s32[2]{0:T(128)S(1)} %pad_add_fusion.where, s32[2,2]{1,0:T(2,128)S(1)} %copy-done.11, bf16[2,256,320]{2,1,0:T(8,128)(2,1)S(1)} %bitcast.34, ...), custom_call_target="tpu_custom_call" | custom-call | flops 943718400 | bytes 6543384 | tf_op jit(solution)/shard_map/one/pallas_call | solution.py:417
  20.9 7.5 %collective-permute-done.2.x = bf16[256,320]{1,0:T(8,128)(2,1)S(1)} collective-permute-done((bf16[256,320]{1,0:T(8,128)(2,1)S(1)}, bf16[256,320]{1,0:T(8,128)(2,1)S(1)}, u32[]{:S(2)}, u32[]{:S(2)}) %collective-permute-start.2) | collective-permute-done | bytes 163872 | tf_op jit(solution)/shard_map/ppermute | solution.py:486
  28.4 8.6 %two.1 = (f32[2,256,320]{2,1,0:T(8,128)S(1)}, f32[2,8,320]{2,1,0:T(8,128)S(1)}, bf16[2,256,320]{2,1,0:T(8,128)(2,1)S(1)}, f32[2,256,320]{2,1,0:T(8,128)S(1)}, f3...) custom-call(s32[2]{0:T(128)S(1)} %pad_add_fusion.where, ...), custom_call_target="tpu_custom_call" | custom-call | flops 1887436800 | bytes 10741784 | tf_op jit(solution)/shard_map/two/pallas_call | solution.py:417
  37.0 1.6 collective-permute-start.4
  38.7 3.6 %collective-permute-done.4.x = bf16[256,320]{1,0:T(8,128)(2,1)S(1)} collective-permute-done((bf16[256,320]{1,0:T(8,128)(2,1)S(1)}, bf16[256,320]{1,0:T(8,128)(2,1)S(1)}, u32[]{:S(2)}, u32[]{:S(2)}) %collective-permute-start.4) | collective-permute-done | bytes 163872 | tf_op jit(solution)/shard_map/ppermute | solution.py:489
  42.2 8.5 %three.1 = (bf16[2,256,320]{2,1,0:T(8,128)(2,1)S(1)}, bf16[2,256,320]{2,1,0:T(8,128)(2,1)S(1)}, bf16[2,256,320]{2,1,0:T(8,128)(2,1)S(1)}, bf16[256,320]{1,0:T(8,128)(2,1)S(1)}) custom-call(s32[2]{0:T(128)S(1)} %pad_add_fusion.where, s32[2,2]{1,0:T(2,128)S(1)} %copy-done.11, bf16[256,320]{1,0:T(8,128)(2,1)S(1)} %collective-permute-done.4.x, ...), custom_call_target="tpu_custom_call" | custom-call | flops 1415577600 | bytes 6686744 | tf_op jit(solution)/shard_map/three/pallas_call | solution.py:417
  52.0 6.3 %collective-permute-done.5.x = bf16[256,320]{1,0:T(8,128)(2,1)S(1)} collective-permute-done((bf16[256,320]{1,0:T(8,128)(2,1)S(1)}, bf16[256,320]{1,0:T(8,128)(2,1)S(1)}, u32[]{:S(2)}, u32[]{:S(2)}) %collective-permute-start.5) | collective-permute-done | bytes 163872 | tf_op jit(solution)/shard_map/ppermute | solution.py:486
  58.3 9.4 %four.1 = (bf16[2,256,320]{2,1,0:T(8,128)(2,1)S(1)}, bf16[2,256,320]{2,1,0:T(8,128)(2,1)S(1)}, bf16[256,320]{1,0:T(8,128)(2,1)S(1)}) custom-call(s32[2]{0:T(128)S(1)} %pad_add_fusion.where, s32[2,2]{1,0:T(2,128)S(1)} %copy-done.11, bf16[256,320]{1,0:T(8,128)(2,1)S(1)} %collective-permute-done.5.x, bf16[2,320,320]{2,1,0:T(8,128)(2,1)S(1)} %bitcast.30, ...), custom_call_target="tpu_custom_call" | custom-call | flops 1887436800 | bytes 10741784 | tf_op jit(solution)/shard_map/four/pallas_call | solution.py:417
  67.7 4.4 %weights.1 = (f32[7680,128]{1,0:T(8,128)S(1)}, bf16[7680,128]{1,0:T(8,128)(2,1)S(1)}) custom-call(s32[2]{0:T(128)S(1)} %pad_add_fusion.where, bf16[2,256,320]{2,1,0:T(8,128)(2,1)S(1)} %get-tuple-element.42.a_hidden, bf16[2,256,320]{2,1,0:T(8,128)(2,1)S(1)} %get-tuple-element.43.a_cots, bf16[2,256,320]{2,1,0:T(8,128)(2,1)S(1)} %get-tuple-element.44.b_hidden, ...), custom_call_target="tpu_custom_call" | custom-call | flops 943718400 | bytes 7208968 | tf_op jit(solution)/shard_map/weights/pallas_call | solution.py:417
  73.7 4.9 %collective-permute-done.6.x = bf16[256,320]{1,0:T(8,128)(2,1)S(1)} collective-permute-done((bf16[256,320]{1,0:T(8,128)(2,1)S(1)}, bf16[256,320]{1,0:T(8,128)(2,1)S(1)}, u32[]{:S(2)}, u32[]{:S(2)}) %collective-permute-start.6) | collective-permute-done | bytes 163872 | tf_op jit(solution)/shard_map/ppermute | solution.py:489
  78.6 6.8 %five.1 = (f32[7680,128]{1,0:T(8,128)S(1)}, bf16[7680,128]{1,0:T(8,128)(2,1)}) custom-call(s32[2]{0:T(128)S(1)} %pad_add_fusion.where, s32[2,2]{1,0:T(2,128)S(1)} %copy-done.12, bf16[256,320]{1,0:T(8,128)(2,1)S(1)} %collective-permute-done.6.x, bf16[2,320,320]{2,1,0:T(8,128)(2,1)S(1)} %bitcast.31, bf16[2,320,320]{2,1,0:T(8,128)(2,1)S(1)} %collective-permute-done.time_other, ...), custom_call_target="tpu_custom_call" | custom-call | flops 1415577600 | bytes 12769304 | tf_op jit(solution)/shard_map/five/pallas_call | solution.py:417
  85.6 2.0 add_convert_fusion
  88.0 4.5 %all-to-all-start.4 = ((bf16[4,1920,128]{2,1,0:T(8,128)(2,1)}), bf16[4,1920,128]{2,1,0:T(8,128)(2,1)S(1)}, u32[]{:S(2)}, u32[]{:S(2)}) async-start(bf16[4,1920,128]{2,1,0:T(8,128)(2,1)} %bitcast.36), calls=%async_computation.4 | async-start | bytes 3932160 | tf_op jit(solution)/shard_map/all_to_all | solution.py:452
  92.6 4.4 %add_convert_fusion.1 = bf16[7680,128]{1,0:T(8,128)(2,1)} fusion(f32[7680,128]{1,0:T(8,128)} %copy-done.8, bf16[7680,128]{1,0:T(8,128)(2,1)} %collective-permute-done.7), kind=kLoop, calls=%fused_computation.1 | loop fusion | flops 2949120 | bytes 7864320 | tf_op jit(solution)/shard_map/convert_element_type | solution.py:453
  97.0 20.5 %all-to-all-done.4 = bf16[4,1920,128]{2,1,0:T(8,128)(2,1)S(1)} async-done(((bf16[4,1920,128]{2,1,0:T(8,128)(2,1)}), bf16[4,1920,128]{2,1,0:T(8,128)(2,1)S(1)}, u32[]{:S(2)}, u32[]{:S(2)}) %all-to-all-start.4) | async-done | bytes 1966112 | tf_op jit(solution)/shard_map/all_to_all | solution.py:452
  117.5 4.4 %all-to-all-start = ((bf16[4,1920,128]{2,1,0:T(8,128)(2,1)}), bf16[4,1920,128]{2,1,0:T(8,128)(2,1)}, u32[]{:S(2)}, u32[]{:S(2)}) async-start(bf16[4,1920,128]{2,1,0:T(8,128)(2,1)} %bitcast.37), calls=%async_computation | async-start | bytes 3932160 | tf_op jit(solution)/shard_map/all_to_all | solution.py:452
  123.1 22.9 %all-to-all-done = bf16[4,1920,128]{2,1,0:T(8,128)(2,1)} async-done(((bf16[4,1920,128]{2,1,0:T(8,128)(2,1)}), bf16[4,1920,128]{2,1,0:T(8,128)(2,1)}, u32[]{:S(2)}, u32[]{:S(2)}) %all-to-all-start) | async-done | bytes 1966112 | tf_op jit(solution)/shard_map/all_to_all | solution.py:452
  146.0 10.1 %all-to-all-start.5 = ((bf16[16,120,128]{2,1,0:T(8,128)(2,1)}), bf16[16,120,128]{2,1,0:T(8,128)(2,1)S(1)}, u32[]{:S(2)}, u32[]{:S(2)}) async-start(bf16[16,120,128]{2,1,0:T(8,128)(2,1)} %bitcast.13), calls=%async_computation.5 | async-start | bytes 983040 | tf_op jit(solution)/shard_map/all_to_all | solution.py:452
  156.1 2.7 reduce_sum.48
  158.8 13.3 %all-to-all-done.5 = bf16[16,120,128]{2,1,0:T(8,128)(2,1)S(1)} async-done(((bf16[16,120,128]{2,1,0:T(8,128)(2,1)}), bf16[16,120,128]{2,1,0:T(8,128)(2,1)S(1)}, u32[]{:S(2)}, u32[]{:S(2)}) %all-to-all-start.5) | async-done | bytes 491552 | tf_op jit(solution)/shard_map/all_to_all | solution.py:452
  172.1 3.6 %all-to-all-start.1 = ((bf16[16,120,128]{2,1,0:T(8,128)(2,1)}), bf16[16,120,128]{2,1,0:T(8,128)(2,1)S(1)}, u32[]{:S(2)}, u32[]{:S(2)}) async-start(bf16[16,120,128]{2,1,0:T(8,128)(2,1)} %bitcast.8), calls=%async_computation.1 | async-start | bytes 983040 | tf_op jit(solution)/shard_map/all_to_all | solution.py:452
  175.8 15.0 %all-to-all-done.1 = bf16[16,120,128]{2,1,0:T(8,128)(2,1)S(1)} async-done(((bf16[16,120,128]{2,1,0:T(8,128)(2,1)}), bf16[16,120,128]{2,1,0:T(8,128)(2,1)S(1)}, u32[]{:S(2)}, u32[]{:S(2)}) %all-to-all-start.1) | async-done | bytes 491552 | tf_op jit(solution)/shard_map/all_to_all | solution.py:452
  191.6 3.6 %all-to-all-start.6 = ((bf16[16,120,128]{2,1,0:T(8,128)(2,1)}), bf16[16,120,128]{2,1,0:T(8,128)(2,1)S(1)}, u32[]{:S(2)}, u32[]{:S(2)}) async-start(bf16[16,120,128]{2,1,0:T(8,128)(2,1)} %broadcast_in_dim.15), calls=%async_computation.6 | async-start | bytes 983040 | tf_op jit(solution)/shard_map/all_to_all | solution.py:461
  195.3 14.5 %all-to-all-done.6 = bf16[16,120,128]{2,1,0:T(8,128)(2,1)S(1)} async-done(((bf16[16,120,128]{2,1,0:T(8,128)(2,1)}), bf16[16,120,128]{2,1,0:T(8,128)(2,1)S(1)}, u32[]{:S(2)}, u32[]{:S(2)}) %all-to-all-start.6) | async-done | bytes 491552 | tf_op jit(solution)/shard_map/all_to_all | solution.py:461
  209.9 17.3 %all_to_all.40 = bf16[16,120,128]{2,1,0:T(8,128)(2,1)S(1)} all-to-all(bf16[16,120,128]{2,1,0:T(8,128)(2,1)S(1)} %broadcast_in_dim.12), channel_id=1, replica_groups=mesh['near'=2,'core'=2,'z'=8,'far'=2,'y'=4] {'z','far'}, dimensions={0} | all-to-all | bytes 983040 | tf_op jit(solution)/shard_map/all_to_all | solution.py:461
  227.4 23.2 %all_to_all.41 = bf16[4,1920,128]{2,1,0:T(8,128)(2,1)} all-to-all(bf16[4,1920,128]{2,1,0:T(8,128)(2,1)S(1)} %broadcast_in_dim.33), channel_id=1, replica_groups=mesh['near'=2,'core'=2,'z'=8,'far'=2,'y'=4] {'y'}, dimensions={0} | all-to-all | bytes 3932160 | tf_op jit(solution)/shard_map/all_to_all | solution.py:461
  252.2 3.6 %all-to-all-start.3 = ((bf16[4,1920,128]{2,1,0:T(8,128)(2,1)}), bf16[4,1920,128]{2,1,0:T(8,128)(2,1)S(1)}, u32[]{:S(2)}, u32[]{:S(2)}) async-start(bf16[4,1920,128]{2,1,0:T(8,128)(2,1)} %broadcast_in_dim.14), calls=%async_computation.3 | async-start | bytes 3932160 | tf_op jit(solution)/shard_map/all_to_all | solution.py:461
  257.3 2.4 unpack.3
  259.7 15.1 %all-to-all-done.3 = bf16[4,1920,128]{2,1,0:T(8,128)(2,1)S(1)} async-done(((bf16[4,1920,128]{2,1,0:T(8,128)(2,1)}), bf16[4,1920,128]{2,1,0:T(8,128)(2,1)S(1)}, u32[]{:S(2)}, u32[]{:S(2)}) %all-to-all-start.3) | async-done | bytes 1966112 | tf_op jit(solution)/shard_map/all_to_all | solution.py:461
  274.8 2.4 unpack.2
  (49 shorter events, 15.7 us)
Async XLA Ops:
  0.6 8.2 %collective-permute-start.1 = (bf16[9,320,320]{2,1,0:T(8,128)(2,1)}, bf16[9,320,320]{2,1,0:T(8,128)(2,1)S(1)}, u32[]{:S(2)}, u32[]{:S(2)}) collective-permute-start(bf16[9,320,320]{2,1,0:T(8,128)(2,1)} %bitcast.17), channel_id=1, source_target_pairs={{0,64},{64,0},{1,65},{65,1},{2,66},{66,2},{3,67},{67,3},{4,68},{68... | collective-permute-start | bytes 5529608 | tf_op jit(solution)/shard_map/ppermute | solution.py:447
  0.7 20.2 %collective-permute-start.3 = (bf16[9,320,320]{2,1,0:T(8,128)(2,1)}, bf16[9,320,320]{2,1,0:T(8,128)(2,1)}, u32[]{:S(2)}, u32[]{:S(2)}) collective-permute-start(bf16[9,320,320]{2,1,0:T(8,128)(2,1)} %bitcast.22), channel_id=1, source_target_pairs={{0,64},{64,0},{1,65},{65,1},{2,66},{66,2},{3,67},{67,3},{4,68},{68... | collective-permute-start | bytes 5529608 | tf_op jit(solution)/shard_map/ppermute | solution.py:447
  1.2 7.6 %collective-permute-start = (bf16[2,320,320]{2,1,0:T(8,128)(2,1)}, bf16[2,320,320]{2,1,0:T(8,128)(2,1)S(1)}, u32[]{:S(2)}, u32[]{:S(2)}) collective-permute-start(bf16[2,320,320]{2,1,0:T(8,128)(2,1)} %bitcast.26), channel_id=1, source_target_pairs={{0,64},{64,0},{1,65},{65,1},{2,66},{66,2},{3,67},{67,3},{4,68},{68... | collective-permute-start | bytes 1228808 | tf_op jit(solution)/shard_map/ppermute | solution.py:447
  8.8 1.6 copy-start
  10.4 1.0 copy-start.3
  11.5 0.9 copy-start.6
  12.4 1.0 copy-start.9
  13.4 0.7 copy-start.11
  14.1 14.3 %copy-start.1 = (bf16[1,3,3,320,320]{4,3,2,1,0:T(8,128)(2,1)S(1)}, bf16[1,3,3,320,320]{4,3,2,1,0:T(8,128)(2,1)}, u32[]{:S(2)}) copy-start(bf16[1,3,3,320,320]{4,3,2,1,0:T(8,128)(2,1)} %param.12) | copy-start | bytes 5529604
  14.1 14.3 %copy-start.2 = (bf16[1,3,3,320,320]{4,3,2,1,0:T(8,128)(2,1)S(1)}, bf16[1,3,3,320,320]{4,3,2,1,0:T(8,128)(2,1)}, u32[]{:S(2)}) copy-start(bf16[1,3,3,320,320]{4,3,2,1,0:T(8,128)(2,1)} %param.13) | copy-start | bytes 5529604
  14.1 14.3 %copy-start.4 = (bf16[1,2,320,320]{3,2,1,0:T(8,128)(2,1)S(1)}, bf16[1,2,320,320]{3,2,1,0:T(8,128)(2,1)}, u32[]{:S(2)}) copy-start(bf16[1,2,320,320]{3,2,1,0:T(8,128)(2,1)} %param.14) | copy-start | bytes 1228804
  14.1 14.4 %copy-start.7 = (bf16[320,320]{1,0:T(8,128)(2,1)S(1)}, bf16[320,320]{1,0:T(8,128)(2,1)}, u32[]{:S(2)}) copy-start(bf16[320,320]{1,0:T(8,128)(2,1)} %constant.25.clone.matrix) | copy-start | bytes 614404
  19.4 22.8 %copy-start.10 = (bf16[2,16,16,320]{3,2,1,0:T(8,128)(2,1)S(1)}, bf16[2,16,16,320]{3,2,1,0:T(8,128)(2,1)}, u32[]{:S(2)}) copy-start(bf16[2,16,16,320]{3,2,1,0:T(8,128)(2,1)} %param.9) | copy-start | bytes 983044
  19.5 9.0 %collective-permute-start.2 = (bf16[256,320]{1,0:T(8,128)(2,1)S(1)}, bf16[256,320]{1,0:T(8,128)(2,1)S(1)}, u32[]{:S(2)}, u32[]{:S(2)}) collective-permute-start(bf16[256,320]{1,0:T(8,128)(2,1)S(1)} %get-tuple-element.25), channel_id=1, source_target_pairs={{0,128},{1,129},{2,130},{3,131},{4,132},{5,133},{6,134},{7,135},{8... | collective-permute-start | bytes 491528 | tf_op jit(solution)/shard_map/ppermute | solution.py:486
  37.0 5.2 %collective-permute-start.4 = (bf16[256,320]{1,0:T(8,128)(2,1)S(1)}, bf16[256,320]{1,0:T(8,128)(2,1)S(1)}, u32[]{:S(2)}, u32[]{:S(2)}) collective-permute-start(bf16[256,320]{1,0:T(8,128)(2,1)S(1)} %get-tuple-element.26), channel_id=1, source_target_pairs={{128,0},{129,1},{130,2},{131,3},{132,4},{133,5},{134,6},{135,7},{1... | collective-permute-start | bytes 491528 | tf_op jit(solution)/shard_map/ppermute | solution.py:489
  50.7 7.6 %collective-permute-start.5 = (bf16[256,320]{1,0:T(8,128)(2,1)S(1)}, bf16[256,320]{1,0:T(8,128)(2,1)S(1)}, u32[]{:S(2)}, u32[]{:S(2)}) collective-permute-start(bf16[256,320]{1,0:T(8,128)(2,1)S(1)} %get-tuple-element.28), channel_id=1, source_target_pairs={{0,128},{1,129},{2,130},{3,131},{4,132},{5,133},{6,134},{7,135},{8... | collective-permute-start | bytes 491528 | tf_op jit(solution)/shard_map/ppermute | solution.py:486
  67.7 10.9 %copy-start.12 = (s32[2,2]{1,0:T(2,128)S(1)}, s32[2,2]{1,0:T(2,128)}, u32[]{:S(2)}) copy-start(s32[2,2]{1,0:T(2,128)} %bucket.9) | copy-start | bytes 52
  72.2 13.4 %collective-permute-start.8 = (bf16[7680,128]{1,0:T(8,128)(2,1)S(1)}, bf16[7680,128]{1,0:T(8,128)(2,1)S(1)}, u32[]{:S(2)}, u32[]{:S(2)}) collective-permute-start(bf16[7680,128]{1,0:T(8,128)(2,1)S(1)} %get-tuple-element.47), channel_id=1, source_target_pairs={{0,64},{64,0},{1,65},{65,1},{2,66},{66,2},{3,67},{67,3},{4,68},{68... | collective-permute-start | bytes 5898248 | tf_op jit(solution)/shard_map/ppermute | solution.py:540
  72.3 6.4 %collective-permute-start.6 = (bf16[256,320]{1,0:T(8,128)(2,1)S(1)}, bf16[256,320]{1,0:T(8,128)(2,1)S(1)}, u32[]{:S(2)}, u32[]{:S(2)}) collective-permute-start(bf16[256,320]{1,0:T(8,128)(2,1)S(1)} %get-tuple-element.33), channel_id=1, source_target_pairs={{128,0},{129,1},{130,2},{131,3},{132,4},{133,5},{134,6},{135,7},{1... | collective-permute-start | bytes 491528 | tf_op jit(solution)/shard_map/ppermute | solution.py:489
  85.5 2.6 copy-start.8
  85.5 7.1 %collective-permute-start.7 = (bf16[7680,128]{1,0:T(8,128)(2,1)}, bf16[7680,128]{1,0:T(8,128)(2,1)}, u32[]{:S(2)}, u32[]{:S(2)}) collective-permute-start(bf16[7680,128]{1,0:T(8,128)(2,1)} %get-tuple-element.41), channel_id=1, source_target_pairs={{0,64},{64,0},{1,65},{65,1},{2,66},{66,2},{3,67},{67,3},{4,68},{68... | collective-permute-start | bytes 5898248 | tf_op jit(solution)/shard_map/ppermute | solution.py:540
  88.0 29.4 %all-to-all-start.4 = ((bf16[4,1920,128]{2,1,0:T(8,128)(2,1)}), bf16[4,1920,128]{2,1,0:T(8,128)(2,1)S(1)}, u32[]{:S(2)}, u32[]{:S(2)}) async-start(bf16[4,1920,128]{2,1,0:T(8,128)(2,1)} %bitcast.36), calls=%async_computation.4 | async-start | bytes 3932160 | tf_op jit(solution)/shard_map/all_to_all | solution.py:452
  117.5 28.5 %all-to-all-start = ((bf16[4,1920,128]{2,1,0:T(8,128)(2,1)}), bf16[4,1920,128]{2,1,0:T(8,128)(2,1)}, u32[]{:S(2)}, u32[]{:S(2)}) async-start(bf16[4,1920,128]{2,1,0:T(8,128)(2,1)} %bitcast.37), calls=%async_computation | async-start | bytes 3932160 | tf_op jit(solution)/shard_map/all_to_all | solution.py:452
  146.0 26.1 %all-to-all-start.5 = ((bf16[16,120,128]{2,1,0:T(8,128)(2,1)}), bf16[16,120,128]{2,1,0:T(8,128)(2,1)S(1)}, u32[]{:S(2)}, u32[]{:S(2)}) async-start(bf16[16,120,128]{2,1,0:T(8,128)(2,1)} %bitcast.13), calls=%async_computation.5 | async-start | bytes 983040 | tf_op jit(solution)/shard_map/all_to_all | solution.py:452
  172.1 18.7 %all-to-all-start.1 = ((bf16[16,120,128]{2,1,0:T(8,128)(2,1)}), bf16[16,120,128]{2,1,0:T(8,128)(2,1)S(1)}, u32[]{:S(2)}, u32[]{:S(2)}) async-start(bf16[16,120,128]{2,1,0:T(8,128)(2,1)} %bitcast.8), calls=%async_computation.1 | async-start | bytes 983040 | tf_op jit(solution)/shard_map/all_to_all | solution.py:452
  191.6 18.2 %all-to-all-start.6 = ((bf16[16,120,128]{2,1,0:T(8,128)(2,1)}), bf16[16,120,128]{2,1,0:T(8,128)(2,1)S(1)}, u32[]{:S(2)}, u32[]{:S(2)}) async-start(bf16[16,120,128]{2,1,0:T(8,128)(2,1)} %broadcast_in_dim.15), calls=%async_computation.6 | async-start | bytes 983040 | tf_op jit(solution)/shard_map/all_to_all | solution.py:461
  252.2 22.6 %all-to-all-start.3 = ((bf16[4,1920,128]{2,1,0:T(8,128)(2,1)}), bf16[4,1920,128]{2,1,0:T(8,128)(2,1)S(1)}, u32[]{:S(2)}, u32[]{:S(2)}) async-start(bf16[4,1920,128]{2,1,0:T(8,128)(2,1)} %broadcast_in_dim.14), calls=%async_computation.3 | async-start | bytes 3932160 | tf_op jit(solution)/shard_map/all_to_all | solution.py:461
  255.8 1.5 copy-start.5
